TPU v7x, 256 devices: a whole 4x4x8 slice. The times are simulated.
256 devices in a mesh: rep: 16 (over z, core), row: 4 (over y), col: 4 (over x).
Axes of the slice: x: 4, y: 4, z: 8, core: 2. Of those that a mesh axis runs over, the one named last changes fastest.
Arguments:
- hidden_in: bfloat16 [16384, 2048], P(('rep', 'row', 'col')), may hold values from -6 to 6
- w_qkv: bfloat16 [2048, 16, 384], P(None, ('row', 'col')), may hold values from -0.125 to 0.125
- w_out: bfloat16 [16, 128, 2048], P(('row', 'col')), may hold values from -0.5 to 0.5
- w_gate_up: bfloat16 [2048, 2, 8192], P(None, None, ('row', 'col')), may hold values from -0.125 to 0.125
- w_down: bfloat16 [8192, 2048], P(('row', 'col')), may hold values from -0.0625 to 0.0625
- cache: bfloat16 [128, 2, 256, 16, 128], P('rep', None, None, ('row', 'col'))
- span_len: int32 [128], replicated, may hold values from 1 to 128, 8192 in all
- cache_len: int32 [128], replicated, may hold values from 1 to 256, 16384 in all
- new_slot: int32 [128], replicated, may hold values from 0 to 127, as said below
Outputs:
- hidden_out: bfloat16 [16384, 2048], P(('rep', 'row', 'col'))
- cache_out: bfloat16 [128, 2, 384, 16, 128], P('rep', None, None, ('row', 'col'))
Inputs may be any that keep to these rules, and one draw needn't show every extreme that they name: A permutation of the 128 slots; slot s lies on replica s // 8, and new_slot[r] mod 8 equals r mod 8; the 8 requests of one replica go to at most 1 slots of any one replica, and some pair of replicas has exactly 1.
All inputs are finite; a program needn't handle non-finite values.
Results may differ from a plain program's by a relative error of at most 0.014.
The roundings to bfloat16 on the way count: a program that leaves them out, or rounds other values in their place, can miss the bound.
Values may be sent and summed in bfloat16 or wider, within the bound.
No kernel may reach another device: no remote copies, remote signals or barrier semaphores. Data moves between devices by JAX's collectives and lax.ppermute only.
A program may use at most 128 MiB of HBM per device.

v0:
```python
import math
import jax
import jax.numpy as jnp
from jax import lax
from jax.sharding import PartitionSpec as P

EPSILON = 1e-05


def layer_norm(values):
    centred = values - jnp.mean(values, axis=-1, keepdims=True)
    spread = jnp.mean(centred * centred, axis=-1, keepdims=True)
    return centred * lax.rsqrt(spread + EPSILON)


def rotate(values, positions):
    halfway = values.shape[-1] // 2
    frequency = 10000.0 ** (-(jnp.arange(halfway, dtype=jnp.float32) * 2.0 / values.shape[-1]))
    angles = positions[..., None] * frequency
    cosine = jnp.cos(angles)
    sine_part = jnp.sin(angles)
    first_half = values[..., :halfway]
    second_half = values[..., halfway:]
    return jnp.concatenate(
        [
            first_half * cosine - second_half * sine_part,
            second_half * cosine + first_half * sine_part,
        ],
        axis=-1,
    )


def attend_one(queries, keys_new, values_new, cache_old, length_old):
    total_keys = jnp.concatenate([cache_old[0], keys_new], axis=0)
    total_values = jnp.concatenate([cache_old[1], values_new], axis=0)
    scores = jnp.einsum("thd,shd->hts", queries, total_keys, preferred_element_type=jnp.float32) * (
        1.0 / math.sqrt(queries.shape[-1])
    )
    source_pos = jnp.arange(total_keys.shape[0], dtype=jnp.int32)
    query_pos = jnp.arange(queries.shape[0], dtype=jnp.int32)
    stored = cache_old.shape[1]
    allowed = jnp.where(
        source_pos[None, :] < stored,
        source_pos[None, :] < length_old,
        source_pos[None, :] - stored <= query_pos[:, None],
    )
    masked_scores = jnp.where(allowed[None], scores, -1e30)
    highest = jnp.max(masked_scores, axis=-1, keepdims=True)
    exponent = jnp.where(allowed[None], jnp.exp(masked_scores - highest), 0.0)
    weights = (exponent / jnp.sum(exponent, axis=-1, keepdims=True)).astype(jnp.bfloat16)
    return jnp.einsum(
        "hts,shd->thd", weights, total_values, preferred_element_type=jnp.float32
    ).astype(jnp.bfloat16)


def assemble_one(old_rows, new_rows, length_old):
    zero_index = jnp.zeros((), jnp.int32)
    extended = jnp.concatenate([old_rows, jnp.zeros_like(new_rows)], axis=1)
    placed = lax.dynamic_update_slice(
        jnp.zeros_like(extended), new_rows, (zero_index, length_old, zero_index, zero_index)
    )
    return extended + placed


def route_tables(new_slot, replica, replicas, slot_count, capacity):
    request_ids = jnp.arange(new_slot.shape[0], dtype=jnp.int32)
    owners = request_ids // slot_count
    targets = new_slot // slot_count
    same_group = (
        (owners[:, None] == owners[None, :])
        & (targets[:, None] == targets[None, :])
        & (request_ids[None, :] < request_ids[:, None])
    )
    ranks = jnp.sum(same_group.astype(jnp.int32), axis=1)
    my_targets = lax.dynamic_slice_in_dim(targets, replica * slot_count, slot_count)
    my_ranks = lax.dynamic_slice_in_dim(ranks, replica * slot_count, slot_count)
    entries = jnp.arange(replicas * capacity, dtype=jnp.int32)
    matches = (my_targets[None, :] == (entries // capacity)[:, None]) & (
        my_ranks[None, :] == (entries % capacity)[:, None]
    )
    send_from = jnp.sum(
        matches.astype(jnp.int32) * jnp.arange(slot_count, dtype=jnp.int32)[None, :], axis=1
    )
    send_live = jnp.any(matches, axis=1)
    my_slots = replica * slot_count + jnp.arange(slot_count, dtype=jnp.int32)
    arrivals = (new_slot[None, :] == my_slots[:, None]).astype(jnp.int32)
    recv_index = jnp.sum(arrivals * (owners * capacity + ranks)[None, :], axis=1)
    return (send_from, send_live, recv_index, arrivals)


def pack_rows(stacked, send_from, send_live):
    taken_rows = jnp.take(stacked, send_from, axis=0)
    live_shape = send_live.reshape((send_live.shape[0],) + (1,) * (stacked.ndim - 1))
    return jnp.where(live_shape, taken_rows, 0.0)


def body(hidden_in, w_qkv, w_out, w_gate_up, w_down, cache, span_len, cache_len, new_slot):
    slot_count = cache.shape[0]
    stored = cache.shape[2]
    heads_here = cache.shape[3]
    head_size = cache.shape[4]
    model_width = hidden_in.shape[1]
    local_rows = hidden_in.shape[0]
    ff_here = w_down.shape[0]
    replica = lax.axis_index("rep")
    replicas = lax.axis_size("rep")
    capacity = (slot_count + replicas - 1) // replicas
    my_cached = lax.dynamic_slice_in_dim(cache_len, replica * slot_count, slot_count)
    my_spans = lax.dynamic_slice_in_dim(span_len, replica * slot_count, slot_count)
    send_from, send_live, recv_index, arrivals = route_tables(
        new_slot, replica, replicas, slot_count, capacity
    )
    stored_rows = jnp.arange(stored, dtype=jnp.int32)
    old_kept = jnp.where(
        (stored_rows[None, :] < my_cached[:, None])[:, None, :, None, None], cache, 0.0
    )
    inputs = hidden_in.astype(jnp.float32)
    normed = layer_norm(inputs).astype(jnp.bfloat16)
    joined = jnp.dot(
        lax.all_gather(normed, ("row", "col"), axis=0, tiled=True),
        w_qkv.reshape(model_width, heads_here * 3 * head_size),
        preferred_element_type=jnp.float32,
    )
    span_rows = joined.shape[0] // slot_count
    joined = joined.reshape(slot_count, span_rows, heads_here, 3, head_size)
    offsets = jnp.arange(span_rows, dtype=jnp.int32)
    positions = (my_cached[:, None] + offsets[None, :]).astype(jnp.float32)[:, :, None]
    queries = rotate(joined[:, :, :, 0], positions).astype(jnp.bfloat16)
    keys_new = rotate(joined[:, :, :, 1], positions).astype(jnp.bfloat16)
    values_new = joined[:, :, :, 2].astype(jnp.bfloat16)
    context = jax.vmap(attend_one)(queries, keys_new, values_new, old_kept, my_cached)
    flat_context = context.reshape(slot_count * span_rows, heads_here * head_size)
    picked = flat_context
    attention = lax.psum_scatter(
        jnp.dot(
            picked,
            w_out.reshape(heads_here * head_size, model_width),
            preferred_element_type=jnp.float32,
        ),
        ("row", "col"),
        scatter_dimension=0,
        tiled=True,
    )
    new_kv = jnp.stack([keys_new, values_new], axis=1)
    new_kept = jnp.where(
        (offsets[None, :] < my_spans[:, None])[:, None, :, None, None], new_kv, 0.0
    )
    appended = jax.vmap(assemble_one)(old_kept, new_kept, my_cached)
    moved_rows = lax.all_to_all(
        pack_rows(appended, send_from, send_live), "rep", split_axis=0, concat_axis=0, tiled=True
    )
    cache_out = jnp.take(moved_rows, recv_index, axis=0)
    middle = (inputs + attention).astype(jnp.bfloat16)
    normed_mid = layer_norm(middle.astype(jnp.float32)).astype(jnp.bfloat16)
    gate_up = jnp.dot(
        lax.all_gather(normed_mid, ("row", "col"), axis=0, tiled=True),
        w_gate_up.reshape(model_width, 2 * ff_here),
        preferred_element_type=jnp.float32,
    )
    hidden = (jax.nn.silu(gate_up[:, :ff_here]) * gate_up[:, ff_here:]).astype(jnp.bfloat16)
    picked = hidden
    down_sum = lax.psum_scatter(
        jnp.dot(picked, w_down, preferred_element_type=jnp.float32).astype(jnp.bfloat16),
        ("row", "col"),
        scatter_dimension=0,
        tiled=True,
    ).astype(jnp.float32)
    row_ids = lax.axis_index(("row", "col")) * local_rows + jnp.arange(local_rows, dtype=jnp.int32)
    slot_of = row_ids // span_rows
    within = row_ids % span_rows
    lengths = jnp.sum(
        jnp.where(
            slot_of[:, None] == jnp.arange(slot_count, dtype=jnp.int32)[None, :],
            my_spans[None, :],
            0,
        ),
        axis=1,
    )
    hidden_out = jnp.where(
        (within < lengths)[:, None], middle.astype(jnp.float32) + down_sum, 0.0
    ).astype(jnp.bfloat16)
    return (hidden_out, cache_out)


def solution(mesh):
    in_specs = (
        P(("rep", "row", "col"), None),
        P(None, ("row", "col"), None),
        P(("row", "col"), None, None),
        P(None, None, ("row", "col")),
        P(("row", "col"), None),
        P("rep", None, None, ("row", "col"), None),
        P(),
        P(),
        P(),
    )
    out_specs = (P(("rep", "row", "col"), None), P("rep", None, None, ("row", "col"), None))
    return jax.shard_map(body, mesh=mesh, in_specs=in_specs, out_specs=out_specs, check_vma=False)
```

profile of v0, /device:TPU:1, one launch (start us, length us, event | category | flops | bytes accessed | tf_op | source)
XLA Modules:
  0.0 450.9 jit_solution(6191463887724648742)
XLA Ops:
  18.2 53.8 %all-gather.3.cloned.1.call-done = bf16[1024,2048]{1,0:T(8,128)(2,1)} async-done(((bf16[64,2048]{1,0:T(8,128)(2,1)}), bf16[1024,2048]{1,0:T(8,128)(2,1)}) %all-gather.3.cloned.1.call-update) | async-done | bytes 4194320 | tf_op jit(solution)/shard_map/all_gather | solution.py:120
  72.0 4.1 convolution_bitcast_fusion
  83.2 3.2 fusion.71
  88.6 4.5 fusion.24
  93.1 88.8 %reduce-scatter.3.cloned.1.call-done = f32[64,2048]{1,0:T(8,128)} async-done(((f32[1024,2048]{1,0:T(8,128)}), f32[64,2048]{1,0:T(8,128)}) %reduce-scatter.3.cloned.1.call-update) | async-done | bytes 524304 | tf_op jit(solution)/shard_map/reduce_scatter | solution.py:134
  185.9 5.4 %copy.76 = bf16[256,8,2,512]{3,1,2,0:T(8,128)(2,1)} copy(bf16[256,8,2,512]{3,2,1,0:T(2,128)(2,1)} %bitcast.121) | data formatting | bytes 8388608
  194.1 48.1 %all-gather.5.cloned.1.call-done = bf16[1024,2048]{1,0:T(8,128)(2,1)} async-done(((bf16[64,2048]{1,0:T(8,128)(2,1)}), bf16[1024,2048]{1,0:T(8,128)(2,1)}) %all-gather.5.cloned.1.call-update) | async-done | bytes 4194320 | tf_op jit(solution)/shard_map/all_gather | solution.py:156
  242.2 7.5 %fusion.74 = f32[1024,1024]{1,0:T(8,128)S(1)} fusion(bf16[1024,2048]{1,0:T(8,128)(2,1)} %all-gather.5.cloned.1.call-done, bf16[2048,1024]{1,0:T(8,128)(2,1)} %bitcast.122), kind=kOutput, calls=%fused_computation.147 | convolution fusion | flops 4294967296 | bytes 12582912 | tf_op jit(solution)/shard_map/dot_general | solution.py:155
  249.7 4.3 convolution_convert_fusion
  255.5 90.9 %while.1 = (s32[]{:T(128)}, bf16[8,2,384,1,128]{4,2,0,3,1:T(8,128)(2,1)}, s32[8,5]{1,0:T(8,128)S(1)}, bf16[8,2,128,1,128]{2,4,0,3,1:T(8,128)(2,1)}, s32[]{:T(128)}, /*index=5*/s32[5]{0:T(128)S(1)}, s32[]{:T(128)}) while((s32[]{:T(128)}, bf16[8,2,384,1,128]{4,2,0,3,1:T(8,128)(2,1)}, s32[8,5]{1,0:T(8,128)S(1)}, bf16[8,2,128,1,128]{2,4,0,3,1:T(8,128)(2,1)}, ...), condition=%wide.while_cond, body=%wide.while_body.sunk | while | flops 32789 | bytes 852227 | solution.py:59
  256.2 3.2 concatenate.79
  264.0 2.9 dynamic-update-slice.3
  267.6 3.2 concatenate.79
  278.9 3.2 concatenate.79
  290.3 3.2 concatenate.79
  301.7 3.2 concatenate.79
  313.0 3.2 concatenate.79
  324.4 3.2 concatenate.79
  335.7 3.2 concatenate.79
  349.3 4.1 gather_fusion
  353.4 4.0 fusion.2
  357.5 7.5 %all-to-all-start = ((bf16[16,2,384,1,128]{4,2,1,3,0:T(8,128)(2,1)}), bf16[16,2,384,1,128]{4,2,1,3,0:T(8,128)(2,1)}, u32[]{:S(2)}, u32[]{:S(2)}) async-start(bf16[16,2,384,1,128]{4,2,1,3,0:T(8,128)(2,1)} %fusion.2), calls=%async_computation.2 | async-start | bytes 6291456 | tf_op jit(solution)/shard_map/all_to_all | solution.py:149
  365.3 70.7 %all-to-all-done = bf16[16,2,384,1,128]{4,2,1,3,0:T(8,128)(2,1)} async-done(((bf16[16,2,384,1,128]{4,2,1,3,0:T(8,128)(2,1)}), bf16[16,2,384,1,128]{4,2,1,3,0:T(8,128)(2,1)}, u32[]{:S(2)}, u32[]{:S(2)}) %all-to-all-start) | async-done | bytes 3145760 | tf_op jit(solution)/shard_map/all_to_all | solution.py:149
  436.1 3.8 gather_fusion.1
  (175 shorter events, 98.4 us)
Async XLA Ops:
  7.2 242.5 %copy-start = (bf16[512,2048]{1,0:T(8,128)(2,1)S(1)}, bf16[512,2048]{1,0:T(8,128)(2,1)}, u32[]{:S(2)}) copy-start(bf16[512,2048]{1,0:T(8,128)(2,1)} %param.13) | copy-start | bytes 6291460
  7.2 64.8 %all-gather.3.cloned.1.call-start = ((), (), s32[]{:S(2)}) async-start(), calls=%async_computation.3 | async-start | bytes 4456448 | tf_op jit(solution)/shard_map/all_gather | solution.py:120
  11.5 170.4 %reduce-scatter.3.cloned.1.call-start = ((), (), s32[]{:S(2)}) async-start(), calls=%async_computation.4 | async-start | bytes 8912896 | tf_op jit(solution)/shard_map/reduce_scatter | solution.py:134
  11.5 3.1 copy-start.9
  78.9 7.6 %copy-start.4 = (bf16[8,128,1,64]{1,3,0,2:T(8,128)(2,1)}, bf16[8,128,1,64]{1,3,0,2:T(8,128)(2,1)S(1)}, u32[]{:S(2)}) copy-start(bf16[8,128,1,64]{1,3,0,2:T(8,128)(2,1)S(1)} %get-tuple-element.62) | copy-start | bytes 393220
  78.9 4.3 copy-start.16
  86.5 2.1 copy-start.7
  93.0 88.9 %copy-start.1 = (bf16[64,2048]{1,0:T(8,128)(2,1)S(1)}, bf16[64,2048]{1,0:T(8,128)(2,1)}, u32[]{:S(2)}) copy-start(bf16[64,2048]{1,0:T(8,128)(2,1)} %param.9) | copy-start | bytes 786436
  93.1 92.8 %copy-start.10 = (s32[128]{0:T(128)S(1)}, s32[128]{0:T(128)}, u32[]{:S(2)}) copy-start(s32[128]{0:T(128)} %param.17) | copy-start | bytes 1540
  93.1 149.1 %all-gather.5.cloned.1.call-start = ((), (), s32[]{:S(2)}) async-start(), calls=%async_computation.5 | async-start | bytes 4456448 | tf_op jit(solution)/shard_map/all_gather | solution.py:156
  183.1 0.7 copy-start.2
  184.7 257.9 %reduce-scatter.5.cloned.1.call-start = ((), (), s32[]{:S(2)}) async-start(), calls=%async_computation.6 | async-start | bytes 4456448 | tf_op jit(solution)/shard_map/reduce_scatter | solution.py:162
  185.7 7.4 %copy-start.14 = (s32[8]{0:T(128)}, s32[8]{0:T(128)S(1)}, u32[]{:S(2)}) copy-start(s32[8]{0:T(128)S(1)} %dynamic_slice.12) | copy-start | bytes 100
  185.9 5.8 %copy-start.8 = (s32[4]{0:T(128)S(1)}, s32[4]{0:T(128)}, u32[]{:S(2)}) copy-start(s32[4]{0:T(128)} %constant.165.clone.1) | copy-start | bytes 52
  185.9 7.2 %copy-start.5 = (bf16[8,128,1,64]{1,3,0,2:T(8,128)(2,1)S(1)}, bf16[8,128,1,64]{1,3,0,2:T(8,128)(2,1)}, u32[]{:S(2)}) copy-start(bf16[8,128,1,64]{1,3,0,2:T(8,128)(2,1)} %copy-done.4) | copy-start | bytes 393220
  185.9 7.2 %copy-start.6 = (bf16[8,1,128,1,128]{2,4,0,3,1:T(8,128)(2,1)S(1)}, bf16[8,1,128,1,128]{2,4,0,3,1:T(8,128)(2,1)}, u32[]{:S(2)}) copy-start(bf16[8,1,128,1,128]{2,4,0,3,1:T(8,128)(2,1)} %get-tuple-element.51) | copy-start | bytes 786436
  254.1 1.5 copy-start.13
  349.3 4.1 copy-start.11
  349.3 4.1 copy-start.12
  357.5 7.8 %copy-start.15 = (s32[8]{0:T(128)S(1)}, s32[8]{0:T(128)}, u32[]{:S(2)}) copy-start(s32[8]{0:T(128)} %copy-done.14) | copy-start | bytes 100
  357.5 78.6 %all-to-all-start = ((bf16[16,2,384,1,128]{4,2,1,3,0:T(8,128)(2,1)}), bf16[16,2,384,1,128]{4,2,1,3,0:T(8,128)(2,1)}, u32[]{:S(2)}, u32[]{:S(2)}) async-start(bf16[16,2,384,1,128]{4,2,1,3,0:T(8,128)(2,1)} %fusion.2), calls=%async_computation.2 | async-start | bytes 6291456 | tf_op jit(solution)/shard_map/all_to_all | solution.py:149
  439.8 2.8 copy-start.3
Sparse Core Ops, SparseCore 0:
  11.6 60.3 all-gather.2
  93.2 88.7 reduce-scatter.2
  184.9 57.1 all-gather.4
  254.2 80.8 reduce-scatter.4
where the time goes:
time: 453 us; the launch traced here: 451 us
  waiting for transfers between devices  262 us (58%)
  local copies, waits for them, and re-layouts  103 us (23%)
  other arithmetic  38.4 us (8%)
  matrix products  25.7 us (6%)
  between operations  14 us (3%)
  starting transfers between devices  7.86 us (2%)
    reduce_scatter x1, waiting for transfers between devices, body(): lax.psum_scatter(jnp.dot(picked, w_out.reshape(heads_here * head_size, mo...  88.8 us
    scatter x64, local copies, waits for them, and re-layouts  78.9 us
    all_to_all x1, waiting for transfers between devices, body(): lax.all_to_all(pack_rows(appended, send_from, send_live), 'rep', split_ax...  70.7 us
    all_gather x1, waiting for transfers between devices, body(): lax.all_gather(normed, ('row', 'col'), axis=0, tiled=True)  53.8 us
    all_gather x1, waiting for transfers between devices, body(): lax.all_gather(normed_mid, ('row', 'col'), axis=0, tiled=True)  48.1 us
    scatter x16, other arithmetic  11.8 us
  transfers between devices with their start and end apart: 5, of which 4 were waited for; matrix products, arithmetic and copies ran while one was open for 28% of the time, Pallas kernels for 0%

commit v1 on v0

--- a/solution.py
+++ b/solution.py
@@ -5,6 +5,27 @@
 from jax.sharding import PartitionSpec as P
 
 EPSILON = 1e-05
+
+
+def gather_around(shard, axis, dim):
+    size, position, extent = (lax.axis_size(axis), lax.axis_index(axis), shard.shape[dim])
+    upward = [(i, (i + 1) % size) for i in range(size)]
+    left = [(i, (i - 1) % size) for i in range(size)]
+    out = jnp.zeros((*shard.shape[:dim], size * extent, *shard.shape[dim + 1 :]), shard.dtype)
+    out = lax.dynamic_update_slice_in_dim(out, shard, position * extent, axis=dim)
+    from_left = from_right = shard
+    halfway = size // 2
+    for step in range(1, halfway + 1):
+        from_left = lax.ppermute(from_left, axis, upward)
+        out = lax.dynamic_update_slice_in_dim(
+            out, from_left, (position - step) % size * extent, axis=dim
+        )
+        if step < size - halfway:
+            from_right = lax.ppermute(from_right, axis, left)
+            out = lax.dynamic_update_slice_in_dim(
+                out, from_right, (position + step) % size * extent, axis=dim
+            )
+    return out
 
 
 def layer_norm(values):
@@ -117,7 +138,7 @@
     inputs = hidden_in.astype(jnp.float32)
     normed = layer_norm(inputs).astype(jnp.bfloat16)
     joined = jnp.dot(
-        lax.all_gather(normed, ("row", "col"), axis=0, tiled=True),
+        gather_around(normed, ("row", "col"), 0),
         w_qkv.reshape(model_width, heads_here * 3 * head_size),
         preferred_element_type=jnp.float32,
     )

time: 453 us -> 474 us (1.046)
  starting transfers between devices: 7.86 us -> 42.8 us
  waiting for transfers between devices: 262 us -> 236 us
  local copies, waits for them, and re-layouts: 103 us -> 116 us
    all_gather x1 -> x0, waiting for transfers between devices: 53.8 us -> none  [body(): lax.all_gather(normed, ('row', 'col'), axis=0, tiled=True)]
    ppermute x0 -> x15, starting transfers between devices: none -> 35 us  [the longest x7 32.9 us: gather_around(): from_right = lax.ppermute(from_right, axis, left)]
    ppermute x0 -> x15, waiting for transfers between devices: none -> 24.5 us  [the longest x8 24.5 us: gather_around(): from_left = lax.ppermute(from_left, axis, upward)]
    dynamic_update_slice x0 -> x15, local copies, waits for them, and re-layouts: none -> 12.8 us  [the longest x8 6.74 us: gather_around(): lax.dynamic_update_slice_in_dim(out, from_left, (position - step) % size...]
  transfers between devices with their start and end apart: 5 -> 19, of which waited for: 4 -> 10; matrix products, arithmetic and copies ran while one was open for 28% -> 28% of each run, Pallas kernels for 0% -> 0%
where the time goes in v1:
time: 474 us; the launch traced here: 471 us
  waiting for transfers between devices  236 us (50%)
  local copies, waits for them, and re-layouts  116 us (24%)
  starting transfers between devices  42.8 us (9%)
  other arithmetic  37.5 us (8%)
  matrix products  25.3 us (5%)
  between operations  14 us (3%)
    reduce_scatter x1, waiting for transfers between devices, body(): lax.psum_scatter(jnp.dot(picked, w_out.reshape(heads_here * head_size, mo...  92.1 us
    scatter x64, local copies, waits for them, and re-layouts  75.4 us
    all_to_all x1, waiting for transfers between devices, body(): lax.all_to_all(pack_rows(appended, send_from, send_live), 'rep', split_ax...  70.7 us
    all_gather x1, waiting for transfers between devices, body(): lax.all_gather(normed_mid, ('row', 'col'), axis=0, tiled=True)  48.3 us
    ppermute x7, starting transfers between devices, gather_around(): from_right = lax.ppermute(from_right, axis, left)  32.9 us
    ppermute x8, waiting for transfers between devices, gather_around(): from_left = lax.ppermute(from_left, axis, upward)  24.5 us
    scatter x16, other arithmetic  11.8 us
  transfers between devices with their start and end apart: 19, of which 10 were waited for; matrix products, arithmetic and copies ran while one was open for 28% of the time, Pallas kernels for 0%

profile of v1, /device:TPU:1, one launch (start us, length us, event | category | flops | bytes accessed | tf_op | source)
XLA Modules:
  0.0 471.2 jit_solution(7824703296546520298)
XLA Ops:
  15.2 3.7 collective-permute-start.1
  25.5 4.8 %collective-permute-start.3 = (bf16[64,2048]{1,0:T(8,128)(2,1)}, bf16[64,2048]{1,0:T(8,128)(2,1)S(1)}, u32[]{:S(2)}, u32[]{:S(2)}) collective-permute-start(bf16[64,2048]{1,0:T(8,128)(2,1)} %collective-permute-done.1), channel_id=1, source_target_pairs={{0,15},{1,0},{2,1},{3,2},{4,3},{5,4},{6,5},{7,6},{8,7},{9,8},{10,9... | collective-permute-start | bytes 786440 | tf_op jit(solution)/shard_map/ppermute | solution.py:24
  34.2 4.8 %collective-permute-start.5 = (bf16[64,2048]{1,0:T(8,128)(2,1)S(1)}, bf16[64,2048]{1,0:T(8,128)(2,1)S(1)}, u32[]{:S(2)}, u32[]{:S(2)}) collective-permute-start(bf16[64,2048]{1,0:T(8,128)(2,1)S(1)} %collective-permute-done.3), channel_id=1, source_target_pairs={{0,15},{1,0},{2,1},{3,2},{4,3},{5,4},{6,5},{7,6},{8,7},{9,8},{10,9... | collective-permute-start | bytes 786440 | tf_op jit(solution)/shard_map/ppermute | solution.py:24
  42.8 4.8 %collective-permute-start.7 = (bf16[64,2048]{1,0:T(8,128)(2,1)S(1)}, bf16[64,2048]{1,0:T(8,128)(2,1)S(1)}, u32[]{:S(2)}, u32[]{:S(2)}) collective-permute-start(bf16[64,2048]{1,0:T(8,128)(2,1)S(1)} %collective-permute-done.5), channel_id=1, source_target_pairs={{0,15},{1,0},{2,1},{3,2},{4,3},{5,4},{6,5},{7,6},{8,7},{9,8},{10,9... | collective-permute-start | bytes 786440 | tf_op jit(solution)/shard_map/ppermute | solution.py:24
  51.3 4.8 %collective-permute-start.9 = (bf16[64,2048]{1,0:T(8,128)(2,1)S(1)}, bf16[64,2048]{1,0:T(8,128)(2,1)S(1)}, u32[]{:S(2)}, u32[]{:S(2)}) collective-permute-start(bf16[64,2048]{1,0:T(8,128)(2,1)S(1)} %collective-permute-done.7), channel_id=1, source_target_pairs={{0,15},{1,0},{2,1},{3,2},{4,3},{5,4},{6,5},{7,6},{8,7},{9,8},{10,9... | collective-permute-start | bytes 786440 | tf_op jit(solution)/shard_map/ppermute | solution.py:24
  59.9 4.9 %collective-permute-start.11 = (bf16[64,2048]{1,0:T(8,128)(2,1)S(1)}, bf16[64,2048]{1,0:T(8,128)(2,1)S(1)}, u32[]{:S(2)}, u32[]{:S(2)}) collective-permute-start(bf16[64,2048]{1,0:T(8,128)(2,1)S(1)} %collective-permute-done.9), channel_id=1, source_target_pairs={{0,15},{1,0},{2,1},{3,2},{4,3},{5,4},{6,5},{7,6},{8,7},{9,8},{10,9... | collective-permute-start | bytes 786440 | tf_op jit(solution)/shard_map/ppermute | solution.py:24
  66.3 3.1 collective-permute-done.10
  69.4 5.1 %collective-permute-start.13 = (bf16[64,2048]{1,0:T(8,128)(2,1)S(1)}, bf16[64,2048]{1,0:T(8,128)(2,1)S(1)}, u32[]{:S(2)}, u32[]{:S(2)}) collective-permute-start(bf16[64,2048]{1,0:T(8,128)(2,1)S(1)} %collective-permute-done.11), channel_id=1, source_target_pairs={{0,15},{1,0},{2,1},{3,2},{4,3},{5,4},{6,5},{7,6},{8,7},{9,8},{10,9... | collective-permute-start | bytes 786440 | tf_op jit(solution)/shard_map/ppermute | solution.py:24
  76.0 4.0 collective-permute-done.12
  81.5 9.8 %collective-permute-done.14 = bf16[64,2048]{1,0:T(8,128)(2,1)S(1)} collective-permute-done((bf16[64,2048]{1,0:T(8,128)(2,1)S(1)}, bf16[64,2048]{1,0:T(8,128)(2,1)S(1)}, u32[]{:S(2)}, u32[]{:S(2)}) %collective-permute-start.14) | collective-permute-done | bytes 262176 | tf_op jit(solution)/shard_map/ppermute | solution.py:19
  92.0 3.6 convolution_bitcast_fusion
  103.5 3.3 fusion.72
  108.9 4.5 fusion.24
  113.4 92.1 %reduce-scatter.3.cloned.1.call-done = f32[64,2048]{1,0:T(8,128)} async-done(((f32[1024,2048]{1,0:T(8,128)}), f32[64,2048]{1,0:T(8,128)}) %reduce-scatter.3.cloned.1.call-update) | async-done | bytes 524304 | tf_op jit(solution)/shard_map/reduce_scatter | solution.py:155
  209.6 5.4 %copy.153 = bf16[256,8,2,512]{3,1,2,0:T(8,128)(2,1)} copy(bf16[256,8,2,512]{3,2,1,0:T(2,128)(2,1)} %bitcast.121) | data formatting | bytes 8388608
  217.7 48.3 %all-gather.2.cloned.1.call-done = bf16[1024,2048]{1,0:T(8,128)(2,1)} async-done(((bf16[64,2048]{1,0:T(8,128)(2,1)}), bf16[1024,2048]{1,0:T(8,128)(2,1)}) %all-gather.2.cloned.1.call-update) | async-done | bytes 4194320 | tf_op jit(solution)/shard_map/all_gather | solution.py:177
  266.0 7.5 %fusion.75 = f32[1024,1024]{1,0:T(8,128)S(1)} fusion(bf16[1024,2048]{1,0:T(8,128)(2,1)} %all-gather.2.cloned.1.call-done, bf16[2048,1024]{1,0:T(8,128)(2,1)} %bitcast.122), kind=kOutput, calls=%fused_computation.163 | convolution fusion | flops 4294967296 | bytes 12582912 | tf_op jit(solution)/shard_map/dot_general | solution.py:176
  273.5 4.4 convolution_convert_fusion
  279.4 87.4 %while.1 = (s32[]{:T(128)}, bf16[8,2,384,1,128]{4,2,0,3,1:T(8,128)(2,1)}, s32[8,5]{1,0:T(8,128)S(1)}, bf16[8,2,128,1,128]{2,4,0,3,1:T(8,128)(2,1)}, s32[]{:T(128)}, /*index=5*/s32[5]{0:T(128)S(1)}, s32[]{:T(128)}) while((s32[]{:T(128)}, bf16[8,2,384,1,128]{4,2,0,3,1:T(8,128)(2,1)}, s32[8,5]{1,0:T(8,128)S(1)}, bf16[8,2,128,1,128]{2,4,0,3,1:T(8,128)(2,1)}, ...), condition=%wide.while_cond, body=%wide.while_body.sunk | while | flops 32789 | bytes 852227 | solution.py:80
  369.7 4.1 gather_fusion
  373.7 4.0 fusion.2
  377.8 7.5 %all-to-all-start = ((bf16[16,2,384,1,128]{4,2,1,3,0:T(8,128)(2,1)}), bf16[16,2,384,1,128]{4,2,1,3,0:T(8,128)(2,1)}, u32[]{:S(2)}, u32[]{:S(2)}) async-start(bf16[16,2,384,1,128]{4,2,1,3,0:T(8,128)(2,1)} %fusion.2), calls=%async_computation.2 | async-start | bytes 6291456 | tf_op jit(solution)/shard_map/all_to_all | solution.py:170
  385.6 70.7 %all-to-all-done = bf16[16,2,384,1,128]{4,2,1,3,0:T(8,128)(2,1)} async-done(((bf16[16,2,384,1,128]{4,2,1,3,0:T(8,128)(2,1)}), bf16[16,2,384,1,128]{4,2,1,3,0:T(8,128)(2,1)}, u32[]{:S(2)}, u32[]{:S(2)}) %all-to-all-start) | async-done | bytes 3145760 | tf_op jit(solution)/shard_map/all_to_all | solution.py:170
  456.4 3.8 gather_fusion.1
  (218 shorter events, 148.0 us)
Async XLA Ops:
  7.2 266.3 %copy-start = (bf16[512,2048]{1,0:T(8,128)(2,1)S(1)}, bf16[512,2048]{1,0:T(8,128)(2,1)}, u32[]{:S(2)}) copy-start(bf16[512,2048]{1,0:T(8,128)(2,1)} %param.13) | copy-start | bytes 6291460
  7.2 11.7 %copy-start.10 = (s32[128]{0:T(128)S(1)}, s32[128]{0:T(128)}, u32[]{:S(2)}) copy-start(s32[128]{0:T(128)} %param.16) | copy-start | bytes 1540
  7.2 198.3 %reduce-scatter.3.cloned.1.call-start = ((), (), s32[]{:S(2)}) async-start(), calls=%async_computation.3 | async-start | bytes 8912896 | tf_op jit(solution)/shard_map/reduce_scatter | solution.py:155
  13.1 12.4 %collective-permute-start = (bf16[64,2048]{1,0:T(8,128)(2,1)}, bf16[64,2048]{1,0:T(8,128)(2,1)}, u32[]{:S(2)}, u32[]{:S(2)}) collective-permute-start(bf16[64,2048]{1,0:T(8,128)(2,1)} %get-tuple-element.47), channel_id=1, source_target_pairs={{0,1},{1,2},{2,3},{3,4},{4,5},{5,6},{6,7},{7,8},{8,9},{9,10},{10,1... | collective-permute-start | bytes 786440 | tf_op jit(solution)/shard_map/ppermute | solution.py:19
  15.2 10.3 %collective-permute-start.1 = (bf16[64,2048]{1,0:T(8,128)(2,1)}, bf16[64,2048]{1,0:T(8,128)(2,1)}, u32[]{:S(2)}, u32[]{:S(2)}) collective-permute-start(bf16[64,2048]{1,0:T(8,128)(2,1)} %get-tuple-element.47), channel_id=1, source_target_pairs={{0,15},{1,0},{2,1},{3,2},{4,3},{5,4},{6,5},{7,6},{8,7},{9,8},{10,9... | collective-permute-start | bytes 786440 | tf_op jit(solution)/shard_map/ppermute | solution.py:24
  25.5 8.8 %collective-permute-start.2 = (bf16[64,2048]{1,0:T(8,128)(2,1)}, bf16[64,2048]{1,0:T(8,128)(2,1)S(1)}, u32[]{:S(2)}, u32[]{:S(2)}) collective-permute-start(bf16[64,2048]{1,0:T(8,128)(2,1)} %collective-permute-done), channel_id=1, source_target_pairs={{0,1},{1,2},{2,3},{3,4},{4,5},{5,6},{6,7},{7,8},{8,9},{9,10},{10,1... | collective-permute-start | bytes 786440 | tf_op jit(solution)/shard_map/ppermute | solution.py:19
  25.5 8.8 %collective-permute-start.3 = (bf16[64,2048]{1,0:T(8,128)(2,1)}, bf16[64,2048]{1,0:T(8,128)(2,1)S(1)}, u32[]{:S(2)}, u32[]{:S(2)}) collective-permute-start(bf16[64,2048]{1,0:T(8,128)(2,1)} %collective-permute-done.1), channel_id=1, source_target_pairs={{0,15},{1,0},{2,1},{3,2},{4,3},{5,4},{6,5},{7,6},{8,7},{9,8},{10,9... | collective-permute-start | bytes 786440 | tf_op jit(solution)/shard_map/ppermute | solution.py:24
  34.2 8.5 %collective-permute-start.4 = (bf16[64,2048]{1,0:T(8,128)(2,1)S(1)}, bf16[64,2048]{1,0:T(8,128)(2,1)S(1)}, u32[]{:S(2)}, u32[]{:S(2)}) collective-permute-start(bf16[64,2048]{1,0:T(8,128)(2,1)S(1)} %collective-permute-done.2), channel_id=1, source_target_pairs={{0,1},{1,2},{2,3},{3,4},{4,5},{5,6},{6,7},{7,8},{8,9},{9,10},{10,1... | collective-permute-start | bytes 786440 | tf_op jit(solution)/shard_map/ppermute | solution.py:19
  34.2 8.5 %collective-permute-start.5 = (bf16[64,2048]{1,0:T(8,128)(2,1)S(1)}, bf16[64,2048]{1,0:T(8,128)(2,1)S(1)}, u32[]{:S(2)}, u32[]{:S(2)}) collective-permute-start(bf16[64,2048]{1,0:T(8,128)(2,1)S(1)} %collective-permute-done.3), channel_id=1, source_target_pairs={{0,15},{1,0},{2,1},{3,2},{4,3},{5,4},{6,5},{7,6},{8,7},{9,8},{10,9... | collective-permute-start | bytes 786440 | tf_op jit(solution)/shard_map/ppermute | solution.py:24
  39.8 52.2 %copy-start.4 = (bf16[2048,1,384]{0,2,1:T(8,128)(2,1)S(1)}, bf16[2048,1,384]{0,2,1:T(8,128)(2,1)}, u32[]{:S(2)}) copy-start(bf16[2048,1,384]{0,2,1:T(8,128)(2,1)} %copy.49) | copy-start | bytes 4718596
  42.8 8.5 %collective-permute-start.6 = (bf16[64,2048]{1,0:T(8,128)(2,1)S(1)}, bf16[64,2048]{1,0:T(8,128)(2,1)S(1)}, u32[]{:S(2)}, u32[]{:S(2)}) collective-permute-start(bf16[64,2048]{1,0:T(8,128)(2,1)S(1)} %collective-permute-done.4), channel_id=1, source_target_pairs={{0,1},{1,2},{2,3},{3,4},{4,5},{5,6},{6,7},{7,8},{8,9},{9,10},{10,1... | collective-permute-start | bytes 786440 | tf_op jit(solution)/shard_map/ppermute | solution.py:19
  42.8 8.5 %collective-permute-start.7 = (bf16[64,2048]{1,0:T(8,128)(2,1)S(1)}, bf16[64,2048]{1,0:T(8,128)(2,1)S(1)}, u32[]{:S(2)}, u32[]{:S(2)}) collective-permute-start(bf16[64,2048]{1,0:T(8,128)(2,1)S(1)} %collective-permute-done.5), channel_id=1, source_target_pairs={{0,15},{1,0},{2,1},{3,2},{4,3},{5,4},{6,5},{7,6},{8,7},{9,8},{10,9... | collective-permute-start | bytes 786440 | tf_op jit(solution)/shard_map/ppermute | solution.py:24
  51.3 8.5 %collective-permute-start.8 = (bf16[64,2048]{1,0:T(8,128)(2,1)S(1)}, bf16[64,2048]{1,0:T(8,128)(2,1)S(1)}, u32[]{:S(2)}, u32[]{:S(2)}) collective-permute-start(bf16[64,2048]{1,0:T(8,128)(2,1)S(1)} %collective-permute-done.6), channel_id=1, source_target_pairs={{0,1},{1,2},{2,3},{3,4},{4,5},{5,6},{6,7},{7,8},{8,9},{9,10},{10,1... | collective-permute-start | bytes 786440 | tf_op jit(solution)/shard_map/ppermute | solution.py:19
  51.3 8.5 %collective-permute-start.9 = (bf16[64,2048]{1,0:T(8,128)(2,1)S(1)}, bf16[64,2048]{1,0:T(8,128)(2,1)S(1)}, u32[]{:S(2)}, u32[]{:S(2)}) collective-permute-start(bf16[64,2048]{1,0:T(8,128)(2,1)S(1)} %collective-permute-done.7), channel_id=1, source_target_pairs={{0,15},{1,0},{2,1},{3,2},{4,3},{5,4},{6,5},{7,6},{8,7},{9,8},{10,9... | collective-permute-start | bytes 786440 | tf_op jit(solution)/shard_map/ppermute | solution.py:24
  59.9 9.6 %collective-permute-start.10 = (bf16[64,2048]{1,0:T(8,128)(2,1)S(1)}, bf16[64,2048]{1,0:T(8,128)(2,1)S(1)}, u32[]{:S(2)}, u32[]{:S(2)}) collective-permute-start(bf16[64,2048]{1,0:T(8,128)(2,1)S(1)} %collective-permute-done.8), channel_id=1, source_target_pairs={{0,1},{1,2},{2,3},{3,4},{4,5},{5,6},{6,7},{7,8},{8,9},{9,10},{10,1... | collective-permute-start | bytes 786440 | tf_op jit(solution)/shard_map/ppermute | solution.py:19
  59.9 9.6 %collective-permute-start.11 = (bf16[64,2048]{1,0:T(8,128)(2,1)S(1)}, bf16[64,2048]{1,0:T(8,128)(2,1)S(1)}, u32[]{:S(2)}, u32[]{:S(2)}) collective-permute-start(bf16[64,2048]{1,0:T(8,128)(2,1)S(1)} %collective-permute-done.9), channel_id=1, source_target_pairs={{0,15},{1,0},{2,1},{3,2},{4,3},{5,4},{6,5},{7,6},{8,7},{9,8},{10,9... | collective-permute-start | bytes 786440 | tf_op jit(solution)/shard_map/ppermute | solution.py:24
  69.4 10.6 %collective-permute-start.12 = (bf16[64,2048]{1,0:T(8,128)(2,1)S(1)}, bf16[64,2048]{1,0:T(8,128)(2,1)S(1)}, u32[]{:S(2)}, u32[]{:S(2)}) collective-permute-start(bf16[64,2048]{1,0:T(8,128)(2,1)S(1)} %collective-permute-done.10), channel_id=1, source_target_pairs={{0,1},{1,2},{2,3},{3,4},{4,5},{5,6},{6,7},{7,8},{8,9},{9,10},{10,1... | collective-permute-start | bytes 786440 | tf_op jit(solution)/shard_map/ppermute | solution.py:19
  69.4 11.4 %collective-permute-start.13 = (bf16[64,2048]{1,0:T(8,128)(2,1)S(1)}, bf16[64,2048]{1,0:T(8,128)(2,1)S(1)}, u32[]{:S(2)}, u32[]{:S(2)}) collective-permute-start(bf16[64,2048]{1,0:T(8,128)(2,1)S(1)} %collective-permute-done.11), channel_id=1, source_target_pairs={{0,15},{1,0},{2,1},{3,2},{4,3},{5,4},{6,5},{7,6},{8,7},{9,8},{10,9... | collective-permute-start | bytes 786440 | tf_op jit(solution)/shard_map/ppermute | solution.py:24
  80.1 11.2 %collective-permute-start.14 = (bf16[64,2048]{1,0:T(8,128)(2,1)S(1)}, bf16[64,2048]{1,0:T(8,128)(2,1)S(1)}, u32[]{:S(2)}, u32[]{:S(2)}) collective-permute-start(bf16[64,2048]{1,0:T(8,128)(2,1)S(1)} %collective-permute-done.12), channel_id=1, source_target_pairs={{0,1},{1,2},{2,3},{3,4},{4,5},{5,6},{6,7},{7,8},{8,9},{9,10},{10,1... | collective-permute-start | bytes 786440 | tf_op jit(solution)/shard_map/ppermute | solution.py:19
  113.4 96.1 %copy-start.11 = (s32[128]{0:T(128)S(1)}, s32[128]{0:T(128)}, u32[]{:S(2)}) copy-start(s32[128]{0:T(128)} %param.17) | copy-start | bytes 1540
  113.4 152.6 %all-gather.2.cloned.1.call-start = ((), (), s32[]{:S(2)}) async-start(), calls=%async_computation.4 | async-start | bytes 4456448 | tf_op jit(solution)/shard_map/all_gather | solution.py:177
  208.3 254.6 %reduce-scatter.5.cloned.1.call-start = ((), (), s32[]{:S(2)}) async-start(), calls=%async_computation.5 | async-start | bytes 4456448 | tf_op jit(solution)/shard_map/reduce_scatter | solution.py:183
  377.8 7.8 %copy-start.16 = (s32[8]{0:T(128)S(1)}, s32[8]{0:T(128)}, u32[]{:S(2)}) copy-start(s32[8]{0:T(128)} %copy-done.15) | copy-start | bytes 100
  377.8 78.6 %all-to-all-start = ((bf16[16,2,384,1,128]{4,2,1,3,0:T(8,128)(2,1)}), bf16[16,2,384,1,128]{4,2,1,3,0:T(8,128)(2,1)}, u32[]{:S(2)}, u32[]{:S(2)}) async-start(bf16[16,2,384,1,128]{4,2,1,3,0:T(8,128)(2,1)} %fusion.2), calls=%async_computation.2 | async-start | bytes 6291456 | tf_op jit(solution)/shard_map/all_to_all | solution.py:170
  (12 other events, 52.4 us)
Sparse Core Ops, SparseCore 0:
  113.5 91.9 reduce-scatter.2
  208.5 57.4 all-gather.1
  278.0 80.7 reduce-scatter.4
